TPU v7x, 512 devices: a whole 4x8x8 slice. The times are simulated.
512 devices in a mesh: segment: 4 (over x), dp: 128 (over y, z, core).
Axes of the slice: x: 4, y: 8, z: 8, core: 2. Of those that a mesh axis runs over, the one named last changes fastest.
Arguments:
- fwd_in: bfloat16 [2, 4, 128, 16, 32, 256], P(None, 'segment', 'dp'), may hold values from -6 to 6
- bwd_in: bfloat16 [4, 4, 128, 16, 32, 256], P(None, 'segment', 'dp'), may hold values from -6 to 6
- fresh: bfloat16 [2, 128, 16, 32, 256], P(None, 'dp'), may hold values from -6 to 6
- top_cot: bfloat16 [2, 128, 16, 32, 256], P(None, 'dp'), may hold values from -6 to 6
- conv_weight: bfloat16 [4, 256, 9, 256], P('segment', 'dp'), may hold values from -0.125 to 0.125
Outputs:
- fwd_out: bfloat16 [2, 4, 128, 16, 32, 256], P(None, 'segment', 'dp')
- bwd_out: bfloat16 [4, 4, 128, 16, 32, 256], P(None, 'segment', 'dp')
- weight_grad: float32 [4, 256, 9, 256], P('segment', 'dp')
All inputs are finite; a program needn't handle non-finite values.
Results may differ from a plain program's by a relative error of at most 0.0055.
Values may be sent and summed in bfloat16 or wider, within the bound.
A program may use at most 64 MiB of HBM per device.

v0:
```python
import jax
import jax.numpy as jnp
from jax import lax
from jax.sharding import PartitionSpec as P


def from_partner(x, axis, bit):
    return lax.ppermute(x, axis, [(i, i ^ 1 << bit) for i in range(lax.axis_size(axis))])


def passed_along(block, axis, distance):
    devices = range(lax.axis_size(axis))
    route = [(i - distance, i) for i in devices if i - distance in devices]
    return lax.ppermute(block, axis, route)


def border_send(tile, parity):
    return jnp.where(parity == 0, tile[:, -1], tile[:, 0])


def extend_rows(tile, received, parity):
    blank_row = jnp.zeros_like(received)
    above_row = jnp.where(parity == 1, received, blank_row)[:, None]
    below_row = jnp.where(parity == 0, received, blank_row)[:, None]
    stacked = jnp.concatenate([above_row, tile, below_row], axis=1)
    return jnp.pad(stacked, ((0, 0), (0, 0), (1, 1), (0, 0)))


def window_at(extended, row_off, col_off, height, width, amount):
    portion = extended[:, row_off : row_off + height, col_off : col_off + width, :]
    return portion.reshape(-1, amount)


def conv_part(extended, weight_piece, height, width):
    amount = weight_piece.shape[0]
    running = None
    for row_off in range(3):
        for col_off in range(3):
            product_term = jnp.dot(
                window_at(extended, row_off, col_off, height, width, amount),
                weight_piece[:, 3 * row_off + col_off, :],
                preferred_element_type=jnp.float32,
            )
            running = product_term if running is None else running + product_term
    return running


def conv_transposed(cot_ext, weight_piece, height, width):
    channels = cot_ext.shape[3]
    running = None
    for row_off in range(3):
        for col_off in range(3):
            window = cot_ext[
                :, 2 - row_off : 2 - row_off + height, 2 - col_off : 2 - col_off + width, :
            ].reshape(-1, channels)
            product_term = lax.dot_general(
                window,
                weight_piece[:, 3 * row_off + col_off, :],
                (((1,), (1,)), ((), ())),
                preferred_element_type=jnp.float32,
            )
            running = product_term if running is None else running + product_term
    return running


def grad_part(extended, cotangent, amount, height, width):
    cot_flat = cotangent.reshape(-1, cotangent.shape[3])
    listing = []
    for row_off in range(3):
        for col_off in range(3):
            window = window_at(extended, row_off, col_off, height, width, amount)
            listing.append(
                lax.dot_general(
                    window, cot_flat, (((0,), (0,)), ((), ())), preferred_element_type=jnp.float32
                )
            )
    return jnp.stack(listing, axis=1)


def shards(fwd_in, bwd_in, fresh, top_cot, conv_weight):
    parity = lax.axis_index("dp") % 2
    segment_pos = lax.axis_index("segment")
    last_segment = lax.axis_size("segment") - 1
    weight_shard = conv_weight[0]
    height = fwd_in.shape[3]
    width = fwd_in.shape[4]
    channels = fwd_in.shape[5]
    pixels_all = lax.axis_size("dp") * height * width
    full_weight = lax.all_gather(weight_shard, "dp", axis=0, tiled=True)

    def two_convs(ext_fwd, ext_rec):
        return (
            conv_part(ext_fwd, full_weight, height, width),
            conv_part(ext_rec, full_weight, height, width),
        )

    def back_conv(cot_ext):
        return conv_transposed(cot_ext, full_weight, height, width)

    def one_step(stream_pair, back_four):
        first_in = stream_pair[0]
        second_in = stream_pair[1]
        out_first = back_four[0]
        out_second = back_four[1]
        cot_first = back_four[2]
        cot_second = back_four[3]
        received = from_partner(
            (
                border_send(second_in, parity),
                border_send(out_first, parity),
                border_send(cot_second, parity),
            ),
            "dp",
            0,
        )
        ext_fwd = jnp.maximum(extend_rows(second_in, received[0], parity), 0)
        ext_rec = jnp.maximum(extend_rows(out_first, received[1], parity), 0)
        ext_cot = extend_rows(cot_second, received[2], parity)
        branch_fwd, branch_rec = two_convs(ext_fwd, ext_rec)
        tile_shape = first_in.shape
        new_second = (first_in.astype(jnp.float32) + branch_fwd.reshape(tile_shape)).astype(
            jnp.bfloat16
        )
        forward_pair = jnp.stack([second_in, new_second])
        rebuilt = (out_second.astype(jnp.float32) - branch_rec.reshape(tile_shape)).astype(
            jnp.bfloat16
        )
        through = back_conv(ext_cot).reshape(tile_shape)
        cot_rebuilt = (
            cot_first.astype(jnp.float32) + jnp.where(out_first > 0, through, 0.0)
        ).astype(jnp.bfloat16)
        message = jnp.stack([rebuilt, out_first, cot_second, cot_rebuilt])
        return (forward_pair, message, (ext_rec, cot_second))

    forward_one, message_one, first_terms = one_step(fwd_in[:, 0], bwd_in[:, 0])
    arrived_fwd = passed_along(forward_one, "segment", 1)
    arrived_back = passed_along(message_one, "segment", -1)
    pair_two = jnp.where(segment_pos == 0, fresh, arrived_fwd)
    four_two = jnp.where(
        segment_pos == last_segment, jnp.concatenate([forward_one, top_cot], axis=0), arrived_back
    )
    forward_two, message_two, second_terms = one_step(pair_two, four_two)
    shard_rows = weight_shard.shape[0]
    summed = lax.psum(
        grad_part(first_terms[0], first_terms[1], channels, height, width)
        + grad_part(second_terms[0], second_terms[1], channels, height, width),
        "dp",
    )
    owned = lax.dynamic_slice_in_dim(summed, lax.axis_index("dp") * shard_rows, shard_rows, 0)
    weight_grad = (owned * (2.0 * pixels_all) ** (-0.5))[None]
    return (forward_two[:, None], message_two[:, None], weight_grad)


def solution(mesh):
    in_specs = (
        P(None, "segment", "dp", None, None, None),
        P(None, "segment", "dp", None, None, None),
        P(None, "dp", None, None, None),
        P(None, "dp", None, None, None),
        P("segment", "dp", None, None),
    )
    out_specs = (
        P(None, "segment", "dp", None, None, None),
        P(None, "segment", "dp", None, None, None),
        P("segment", "dp", None, None),
    )
    return jax.shard_map(shards, mesh=mesh, in_specs=in_specs, out_specs=out_specs, check_vma=False)
```

profile of v0, /device:TPU:24, one launch (start us, length us, event | category | flops | bytes accessed | tf_op | source)
XLA Modules:
  0.0 387.7 jit_solution(14345244486883992187)
XLA Ops:
  7.2 1.4 copy.35
  8.7 1.8 slice_bitcast_fusion.4
  10.5 1.9 collective-permute-start
  12.5 1.0 slice_bitcast_fusion.3
  13.4 2.4 collective-permute-start.3
  15.9 1.9 collective-permute-start.4
  18.9 0.8 pad_maximum_fusion.4
  19.7 1.0 fusion.18
  20.7 1.0 fusion.17
  22.0 1.0 fusion.16
  23.0 1.0 fusion.15
  23.9 1.0 fusion.14
  24.9 1.0 fusion.13
  25.9 1.0 fusion.12
  26.9 1.0 fusion.11
  27.9 1.0 fusion.10
  28.8 1.2 fusion.45
  30.0 1.5 fusion.47
  31.5 67.2 %all-gather.3.cloned.1.call-done = bf16[1,256,9,256]{3,2,0,1:T(8,128)(2,1)} async-done(((bf16[1,2,9,256]{3,2,0,1:T(8,128)(2,1)}), bf16[1,256,9,256]{3,2,0,1:T(8,128)(2,1)}) %all-gather.3.cloned.1.call-update) | async-done | bytes 1179664 | tf_op jit(solution)/shard_map/all_gather | solution.py:89
  98.7 2.0 copy.51
  101.3 0.6 copy-done.17
  110.6 3.5 collective-permute-start.1
  115.3 0.7 copy-done.6
  116.2 9.5 %collective-permute-done.1 = bf16[2,1,16,32,256]{4,3,2,1,0:T(8,128)(2,1)S(1)} collective-permute-done((bf16[2,1,16,32,256]{4,3,2,1,0:T(8,128)(2,1)S(1)}, bf16[2,1,16,32,256]{4,3,2,1,0:T(8,128)(2,1)S(1)}, u32[]{:S(2)}, u32[]{:S(2)}) %collective-permute-start.1) | collective-permute-done | bytes 524320 | tf_op jit(solution)/shard_map/ppermute | solution.py:14
  125.8 1.9 collective-permute-start.2
  127.9 1.3 collective-permute-start.5
  132.0 0.8 maximum_bitcast_fusion.1
  132.8 23.3 %collective-permute-done.5 = bf16[4,1,16,32,256]{4,3,2,0,1:T(8,128)(2,1)S(1)} collective-permute-done((bf16[4,1,16,32,256]{4,3,2,0,1:T(8,128)(2,1)S(1)}, bf16[4,1,16,32,256]{4,3,2,0,1:T(8,128)(2,1)S(1)}, u32[]{:S(2)}, u32[]{:S(2)}) %collective-permute-start.5) | collective-permute-done | bytes 1048608 | tf_op jit(solution)/shard_map/ppermute | solution.py:14
  156.3 0.7 slice_bitcast_fusion.1
  157.0 1.9 collective-permute-start.7
  159.0 2.6 collective-permute-start.6
  161.7 1.1 fusion.43
  163.3 0.9 pad_maximum_fusion.2
  165.8 1.1 convolution_add_fusion.13
  167.2 1.1 convolution_add_fusion.12
  168.6 1.1 convolution_add_fusion.11
  170.0 1.1 convolution_add_fusion.10
  171.4 1.1 convolution_add_fusion.9
  172.8 1.1 convolution_add_fusion.8
  174.3 1.9 convolution_add_fusion.7
  176.5 3.4 add.257
  179.9 1.2 copy-done.1
  181.2 1.3 convolution_add_fusion.6
  183.3 0.7 copy-done.8
  185.5 0.7 copy-done.28
  186.2 1.1 maximum_bitcast_fusion
  187.3 192.1 %all-reduce.8.cloned.1.call-done = f32[256,9,256]{2,0,1:T(8,128)} async-done(((f32[256,9,256]{2,0,1:T(8,128)}), f32[256,9,256]{2,0,1:T(8,128)}) %all-reduce.8.cloned.1.call-update) | async-done | bytes 2359312 | tf_op jit(solution)/shard_map/psum | solution.py:144
  379.4 1.5 multiply_bitcast_fusion
  (157 shorter events, 21.3 us)
Async XLA Ops:
  7.2 5.3 %copy-start.5 = (bf16[4,1,1,16,32,256]{5,4,3,2,1,0:T(8,128)(2,1)S(1)}, bf16[4,1,1,16,32,256]{5,4,3,2,1,0:T(8,128)(2,1)}, u32[]{:S(2)}) copy-start(bf16[4,1,1,16,32,256]{5,4,3,2,1,0:T(8,128)(2,1)} %param.6) | copy-start | bytes 3145732
  7.2 91.6 %all-gather.3.cloned.1.call-start = ((), (), s32[]{:S(2)}) async-start(), calls=%async_computation.1 | async-start | bytes 2113536 | tf_op jit(solution)/shard_map/all_gather | solution.py:89
  8.6 370.8 %all-reduce.8.cloned.1.call-start = ((), (), s32[]{:S(2)}) async-start(), calls=%async_computation | async-start | bytes 4718592 | tf_op jit(solution)/shard_map/psum | solution.py:144
  10.5 11.3 %collective-permute-start = (bf16[1,32,256]{2,1,0:T(8,128)(2,1)S(1)}, bf16[1,32,256]{2,1,0:T(8,128)(2,1)S(1)}, u32[]{:S(2)}, u32[]{:S(2)}) collective-permute-start(bf16[1,32,256]{2,1,0:T(8,128)(2,1)S(1)} %fusion.39), channel_id=1, source_target_pairs={{0,1},{1,0},{2,3},{3,2},{4,5},{5,4},{6,7},{7,6},{8,9},{9,8},{10,11... | collective-permute-start | bytes 49160 | tf_op jit(solution)/shard_map/ppermute | solution.py:8
  13.4 4.4 %collective-permute-start.3 = (bf16[1,32,256]{2,1,0:T(8,128)(2,1)S(1)}, bf16[1,32,256]{2,1,0:T(8,128)(2,1)S(1)}, u32[]{:S(2)}, u32[]{:S(2)}) collective-permute-start(bf16[1,32,256]{2,1,0:T(8,128)(2,1)S(1)} %fusion.37), channel_id=1, source_target_pairs={{0,1},{1,0},{2,3},{3,2},{4,5},{5,4},{6,7},{7,6},{8,9},{9,8},{10,11... | collective-permute-start | bytes 49160 | tf_op jit(solution)/shard_map/ppermute | solution.py:8
  15.9 3.1 collective-permute-start.4
  18.3 3.4 copy-start.2
  100.8 64.5 %copy-start = (bf16[1,256,9,256]{3,1,2,0:T(8,128)(2,1)}, bf16[1,256,9,256]{3,1,2,0:T(8,128)(2,1)S(1)}, u32[]{:S(2)}) copy-start(bf16[1,256,9,256]{3,1,2,0:T(8,128)(2,1)S(1)} %copy.51) | copy-start | bytes 3538948
  100.8 1.1 copy-start.17
  101.0 1.2 copy-start.24
  101.9 1.0 copy-start.23
  102.9 0.9 copy-start.3
  105.4 1.0 copy-start.22
  105.7 1.0 copy-start.21
  106.4 1.0 copy-start.20
  106.7 1.0 copy-start.19
  107.4 1.0 copy-start.18
  107.6 1.0 copy-start.16
  108.3 1.0 copy-start.15
  108.6 1.0 copy-start.14
  109.3 1.1 copy-start.31
  109.6 1.0 copy-start.27
  109.8 4.4 %copy-start.13 = (bf16[1,16,32,256]{3,2,1,0:T(8,128)(2,1)S(1)}, bf16[1,16,32,256]{3,2,1,0:T(8,128)(2,1)}, u32[]{:S(2)}) copy-start(bf16[1,16,32,256]{3,2,1,0:T(8,128)(2,1)} %get-tuple-element.47) | copy-start | bytes 786436
  110.6 3.9 %copy-start.12 = (bf16[1,16,32,256]{3,2,1,0:T(8,128)(2,1)S(1)}, bf16[1,16,32,256]{3,2,1,0:T(8,128)(2,1)}, u32[]{:S(2)}) copy-start(bf16[1,16,32,256]{3,2,1,0:T(8,128)(2,1)} %get-tuple-element.46) | copy-start | bytes 786436
  110.6 15.1 %collective-permute-start.1 = (bf16[2,1,16,32,256]{4,3,2,1,0:T(8,128)(2,1)S(1)}, bf16[2,1,16,32,256]{4,3,2,1,0:T(8,128)(2,1)S(1)}, u32[]{:S(2)}, u32[]{:S(2)}) collective-permute-start(bf16[2,1,16,32,256]{4,3,2,1,0:T(8,128)(2,1)S(1)} %pad_maximum_fusion.1), channel_id=1, source_target_pairs={{0,128},{128,256},{256,384},{1,129},{129,257},{257,385},{2,130},{1... | collective-permute-start | bytes 1572872 | tf_op jit(solution)/shard_map/ppermute | solution.py:14
  114.7 1.2 copy-start.6
  115.9 9.7 %copy-start.30 = (bf16[2,1,16,32,256]{4,3,2,1,0:T(8,128)(2,1)S(1)}, bf16[2,1,16,32,256]{4,3,2,1,0:T(8,128)(2,1)}, u32[]{:S(2)}) copy-start(bf16[2,1,16,32,256]{4,3,2,1,0:T(8,128)(2,1)} %param.7) | copy-start | bytes 1572868
  116.2 11.5 %copy-start.25 = (bf16[1,1,16,32,256]{4,3,2,0,1:T(8,128)(2,1)S(1)}, bf16[1,1,16,32,256]{4,3,2,0,1:T(8,128)(2,1)}, u32[]{:S(2)}) copy-start(bf16[1,1,16,32,256]{4,3,2,0,1:T(8,128)(2,1)} %get-tuple-element.12) | copy-start | bytes 786436
  116.2 11.5 %copy-start.26 = (bf16[1,1,16,32,256]{4,3,2,0,1:T(8,128)(2,1)S(1)}, bf16[1,1,16,32,256]{4,3,2,0,1:T(8,128)(2,1)}, u32[]{:S(2)}) copy-start(bf16[1,1,16,32,256]{4,3,2,0,1:T(8,128)(2,1)} %get-tuple-element.14) | copy-start | bytes 786436
  125.8 3.4 collective-permute-start.2
  127.9 28.2 %collective-permute-start.5 = (bf16[4,1,16,32,256]{4,3,2,0,1:T(8,128)(2,1)S(1)}, bf16[4,1,16,32,256]{4,3,2,0,1:T(8,128)(2,1)S(1)}, u32[]{:S(2)}, u32[]{:S(2)}) collective-permute-start(bf16[4,1,16,32,256]{4,3,2,0,1:T(8,128)(2,1)S(1)} %pad_maximum_fusion), channel_id=1, source_target_pairs={{128,0},{256,128},{384,256},{129,1},{257,129},{385,257},{130,2},{2... | collective-permute-start | bytes 3145736 | tf_op jit(solution)/shard_map/ppermute | solution.py:14
  131.8 24.3 %copy-start.29 = (bf16[1,1,16,32,256]{4,3,2,0,1:T(8,128)(2,1)S(1)}, bf16[1,1,16,32,256]{4,3,2,0,1:T(8,128)(2,1)}, u32[]{:S(2)}) copy-start(bf16[1,1,16,32,256]{4,3,2,0,1:T(8,128)(2,1)} %get-tuple-element.16) | copy-start | bytes 786436
  131.8 24.2 %copy-start.32 = (bf16[2,1,16,32,256]{4,3,2,1,0:T(8,128)(2,1)S(1)}, bf16[2,1,16,32,256]{4,3,2,1,0:T(8,128)(2,1)}, u32[]{:S(2)}) copy-start(bf16[2,1,16,32,256]{4,3,2,1,0:T(8,128)(2,1)} %param.8) | copy-start | bytes 1572868
  157.0 4.5 %collective-permute-start.7 = (bf16[1,32,256]{2,1,0:T(8,128)(2,1)S(1)}, bf16[1,32,256]{2,1,0:T(8,128)(2,1)S(1)}, u32[]{:S(2)}, u32[]{:S(2)}) collective-permute-start(bf16[1,32,256]{2,1,0:T(8,128)(2,1)S(1)} %fusion.34), channel_id=1, source_target_pairs={{0,1},{1,0},{2,3},{3,2},{4,5},{5,4},{6,7},{7,6},{8,9},{9,8},{10,11... | collective-permute-start | bytes 49160 | tf_op jit(solution)/shard_map/ppermute | solution.py:8
  159.0 5.3 %collective-permute-start.6 = (bf16[1,32,256]{2,1,0:T(8,128)(2,1)S(1)}, bf16[1,32,256]{2,1,0:T(8,128)(2,1)S(1)}, u32[]{:S(2)}, u32[]{:S(2)}) collective-permute-start(bf16[1,32,256]{2,1,0:T(8,128)(2,1)S(1)} %fusion.35), channel_id=1, source_target_pairs={{0,1},{1,0},{2,3},{3,2},{4,5},{5,4},{6,7},{7,6},{8,9},{9,8},{10,11... | collective-permute-start | bytes 49160 | tf_op jit(solution)/shard_map/ppermute | solution.py:8
  179.9 1.3 copy-start.1
  179.9 2.5 copy-start.11
  181.2 1.5 copy-start.9
  183.0 1.0 copy-start.8
  183.3 1.0 copy-start.10
  183.9 1.0 copy-start.7
  184.2 1.1 copy-start.4
  185.3 0.9 copy-start.28
Sparse Core Ops, SparseCore 0:
  11.7 87.0 all-gather.2
  180.0 199.3 all-reduce.7
where the time goes:
time: 389 us; the launch traced here: 388 us
  waiting for transfers between devices  293 us (75%)
  matrix products  32.2 us (8%)
  local copies, waits for them, and re-layouts  19.8 us (5%)
  starting transfers between devices  17.6 us (5%)
  between operations  15 us (4%)
  other arithmetic  10.5 us (3%)
    psum x1, waiting for transfers between devices, shards(): lax.psum(grad_part(first_terms[0], first_terms[1], channels, height, widt...  192 us
    all_gather x1, waiting for transfers between devices, shards(): full_weight = lax.all_gather(weight_shard, 'dp', axis=0, tiled=True)  67.2 us
    ppermute x2, waiting for transfers between devices, passed_along(): return lax.ppermute(block, axis, route)  32.8 us
    dot_general x36, matrix products, conv_part(): jnp.dot(window_at(extended, row_off, col_off, height, width, amount), wei...  15.3 us
    ppermute x6, starting transfers between devices, from_partner(): lax.ppermute(x, axis, [(i, i ^ 1 << bit) for i in range(lax.axis_size(axi...  12.6 us
    dot_general x18, matrix products, grad_part(): lax.dot_general(window, cot_flat, (((0,), (0,)), ((), ())), preferred_ele...  11.3 us
    unnamed x67, local copies, waits for them, and re-layouts  9.48 us
  transfers between devices with their start and end apart: 10, of which 5 were waited for; matrix products, arithmetic and copies ran while one was open for 7% of the time, Pallas kernels for 0%

commit v1 on v0

--- a/solution.py
+++ b/solution.py
@@ -86,7 +86,9 @@
     width = fwd_in.shape[4]
     channels = fwd_in.shape[5]
     pixels_all = lax.axis_size("dp") * height * width
-    full_weight = lax.all_gather(weight_shard, "dp", axis=0, tiled=True)
+    full_weight = jnp.concatenate(
+        lax.all_to_all(jnp.stack([weight_shard] * lax.axis_size("dp")), "dp", 0, 0), axis=0
+    )
 
     def two_convs(ext_fwd, ext_rec):
         return (

time: 389 us -> 353 us (0.907)
  waiting for transfers between devices: 293 us -> 234 us
  starting transfers between devices: 17.6 us -> 35.5 us
    all_gather x1 -> x0, waiting for transfers between devices: 67.2 us -> none  [shards(): full_weight = lax.all_gather(weight_shard, 'dp', axis=0, tiled=True)]
    all_to_all x0 -> x1, starting transfers between devices: none -> 17.6 us  [shards(): lax.all_to_all(jnp.stack([weight_shard] * lax.axis_size('dp')), 'dp', 0, 0)]
    all_to_all x0 -> x1, waiting for transfers between devices: none -> 11.9 us  [shards(): lax.all_to_all(jnp.stack([weight_shard] * lax.axis_size('dp')), 'dp', 0, 0)]
    unnamed x67 -> x96, local copies, waits for them, and re-layouts: 9.48 us -> 10.1 us
  transfers between devices with their start and end apart: 10 -> 10, of which waited for: 5 -> 5; matrix products, arithmetic and copies ran while one was open for 7% -> 8% of each run, Pallas kernels for 0% -> 0%
where the time goes in v1:
time: 353 us; the launch traced here: 352 us
  waiting for transfers between devices  234 us (66%)
  starting transfers between devices  35.5 us (10%)
  matrix products  33.4 us (9%)
  local copies, waits for them, and re-layouts  22.5 us (6%)
  between operations  15.1 us (4%)
  other arithmetic  10.7 us (3%)
    psum x1, waiting for transfers between devices, shards(): lax.psum(grad_part(first_terms[0], first_terms[1], channels, height, widt...  190 us
    ppermute x2, waiting for transfers between devices, passed_along(): return lax.ppermute(block, axis, route)  32.3 us
    all_to_all x1, starting transfers between devices, shards(): lax.all_to_all(jnp.stack([weight_shard] * lax.axis_size('dp')), 'dp', 0, 0)  17.6 us
    dot_general x36, matrix products, conv_part(): jnp.dot(window_at(extended, row_off, col_off, height, width, amount), wei...  15.3 us
    ppermute x6, starting transfers between devices, from_partner(): lax.ppermute(x, axis, [(i, i ^ 1 << bit) for i in range(lax.axis_size(axi...  12.8 us
    all_to_all x1, waiting for transfers between devices, shards(): lax.all_to_all(jnp.stack([weight_shard] * lax.axis_size('dp')), 'dp', 0, 0)  11.9 us
    dot_general x18, matrix products, grad_part(): lax.dot_general(window, cot_flat, (((0,), (0,)), ((), ())), preferred_ele...  11.2 us
    unnamed x96, local copies, waits for them, and re-layouts  10.1 us
  transfers between devices with their start and end apart: 10, of which 5 were waited for; matrix products, arithmetic and copies ran while one was open for 8% of the time, Pallas kernels for 0%

profile of v1, /device:TPU:24, one launch (start us, length us, event | category | flops | bytes accessed | tf_op | source)
XLA Modules:
  0.0 351.6 jit_solution(8918057782934696423)
XLA Ops:
  7.2 1.8 slice_bitcast_fusion.4
  9.0 0.7 copy-done.17
  9.7 1.9 collective-permute-start
  11.6 2.4 stack.81
  14.0 17.6 %all-to-all-start = ((bf16[128,2,9,256]{3,1,2,0:T(2,128)(2,1)}), bf16[128,2,9,256]{3,1,2,0:T(2,128)(2,1)S(1)}, u32[]{:S(2)}, u32[]{:S(2)}) async-start(bf16[128,2,9,256]{3,1,2,0:T(2,128)(2,1)} %stack.81), calls=%async_computation | async-start | bytes 2359296 | tf_op jit(solution)/shard_map/all_to_all | solution.py:90
  31.6 1.0 slice_bitcast_fusion.3
  32.6 2.0 collective-permute-start.3
  34.6 2.3 collective-permute-start.4
  37.8 1.0 pad_maximum_fusion.4
  38.8 1.0 fusion.18
  39.8 1.0 fusion.17
  41.1 1.0 fusion.16
  42.1 1.0 fusion.15
  43.1 1.0 fusion.14
  44.1 1.0 fusion.13
  45.0 1.0 fusion.12
  46.0 1.0 fusion.11
  47.0 1.0 fusion.10
  48.0 1.3 fusion.45
  49.3 1.6 fusion.47
  50.9 11.9 %all-to-all-done = bf16[128,2,9,256]{3,1,2,0:T(2,128)(2,1)S(1)} async-done(((bf16[128,2,9,256]{3,1,2,0:T(2,128)(2,1)}), bf16[128,2,9,256]{3,1,2,0:T(2,128)(2,1)S(1)}, u32[]{:S(2)}, u32[]{:S(2)}) %all-to-all-start) | async-done | bytes 1179680 | tf_op jit(solution)/shard_map/all_to_all | solution.py:90
  62.8 0.9 copy.35
  64.5 1.4 fusion.29
  76.2 3.6 %collective-permute-start.1 = (bf16[2,1,16,32,256]{4,3,2,1,0:T(8,128)(2,1)S(1)}, bf16[2,1,16,32,256]{4,3,2,1,0:T(8,128)(2,1)S(1)}, u32[]{:S(2)}, u32[]{:S(2)}) collective-permute-start(bf16[2,1,16,32,256]{4,3,2,1,0:T(8,128)(2,1)S(1)} %pad_maximum_fusion.1), channel_id=1, source_target_pairs={{0,128},{128,256},{256,384},{1,129},{129,257},{257,385},{2,130},{1... | collective-permute-start | bytes 1572872 | tf_op jit(solution)/shard_map/ppermute | solution.py:14
  82.1 9.6 %collective-permute-done.1 = bf16[2,1,16,32,256]{4,3,2,1,0:T(8,128)(2,1)S(1)} collective-permute-done((bf16[2,1,16,32,256]{4,3,2,1,0:T(8,128)(2,1)S(1)}, bf16[2,1,16,32,256]{4,3,2,1,0:T(8,128)(2,1)S(1)}, u32[]{:S(2)}, u32[]{:S(2)}) %collective-permute-start.1) | collective-permute-done | bytes 524320 | tf_op jit(solution)/shard_map/ppermute | solution.py:14
  91.9 2.3 collective-permute-start.2
  94.3 1.5 collective-permute-start.5
  98.6 0.8 maximum_bitcast_fusion.1
  99.4 22.7 %collective-permute-done.5 = bf16[4,1,16,32,256]{4,3,2,0,1:T(8,128)(2,1)S(1)} collective-permute-done((bf16[4,1,16,32,256]{4,3,2,0,1:T(8,128)(2,1)S(1)}, bf16[4,1,16,32,256]{4,3,2,0,1:T(8,128)(2,1)S(1)}, u32[]{:S(2)}, u32[]{:S(2)}) %collective-permute-start.5) | collective-permute-done | bytes 1048608 | tf_op jit(solution)/shard_map/ppermute | solution.py:14
  122.4 0.7 slice_bitcast_fusion.1
  123.1 1.9 collective-permute-start.7
  125.0 2.4 collective-permute-start.6
  127.6 1.2 fusion.43
  129.3 0.8 pad_maximum_fusion.2
  131.7 1.1 convolution_add_fusion.13
  133.1 1.1 convolution_add_fusion.12
  134.5 1.1 convolution_add_fusion.11
  135.9 1.1 convolution_add_fusion.10
  137.4 1.1 convolution_add_fusion.9
  138.8 1.1 convolution_add_fusion.8
  140.2 1.9 convolution_add_fusion.7
  142.4 3.4 add.257
  145.9 1.2 copy-done.1
  147.1 1.3 convolution_add_fusion.6
  151.4 0.7 copy-done.43
  152.2 1.1 maximum_bitcast_fusion
  153.3 190.0 %all-reduce.8.cloned.1.call-done = f32[256,9,256]{2,0,1:T(8,128)} async-done(((f32[256,9,256]{2,0,1:T(8,128)}), f32[256,9,256]{2,0,1:T(8,128)}) %all-reduce.8.cloned.1.call-update) | async-done | bytes 2359312 | tf_op jit(solution)/shard_map/psum | solution.py:146
  343.3 1.5 multiply_bitcast_fusion
  (187 shorter events, 24.4 us)
Async XLA Ops:
  9.7 31.2 %collective-permute-start = (bf16[1,32,256]{2,1,0:T(8,128)(2,1)S(1)}, bf16[1,32,256]{2,1,0:T(8,128)(2,1)S(1)}, u32[]{:S(2)}, u32[]{:S(2)}) collective-permute-start(bf16[1,32,256]{2,1,0:T(8,128)(2,1)S(1)} %fusion.39), channel_id=1, source_target_pairs={{0,1},{1,0},{2,3},{3,2},{4,5},{5,4},{6,7},{7,6},{8,9},{9,8},{10,11... | collective-permute-start | bytes 49160 | tf_op jit(solution)/shard_map/ppermute | solution.py:8
  14.0 17.6 %copy-start.15 = (bf16[4,1,1,16,32,256]{5,4,3,2,1,0:T(8,128)(2,1)S(1)}, bf16[4,1,1,16,32,256]{5,4,3,2,1,0:T(8,128)(2,1)}, u32[]{:S(2)}) copy-start(bf16[4,1,1,16,32,256]{5,4,3,2,1,0:T(8,128)(2,1)} %param.6) | copy-start | bytes 3145732
  14.0 48.8 %all-to-all-start = ((bf16[128,2,9,256]{3,1,2,0:T(2,128)(2,1)}), bf16[128,2,9,256]{3,1,2,0:T(2,128)(2,1)S(1)}, u32[]{:S(2)}, u32[]{:S(2)}) async-start(bf16[128,2,9,256]{3,1,2,0:T(2,128)(2,1)} %stack.81), calls=%async_computation | async-start | bytes 2359296 | tf_op jit(solution)/shard_map/all_to_all | solution.py:90
  31.6 311.7 %all-reduce.8.cloned.1.call-start = ((), (), s32[]{:S(2)}) async-start(), calls=%async_computation.1 | async-start | bytes 4718592 | tf_op jit(solution)/shard_map/psum | solution.py:146
  32.6 4.4 %collective-permute-start.3 = (bf16[1,32,256]{2,1,0:T(8,128)(2,1)S(1)}, bf16[1,32,256]{2,1,0:T(8,128)(2,1)S(1)}, u32[]{:S(2)}, u32[]{:S(2)}) collective-permute-start(bf16[1,32,256]{2,1,0:T(8,128)(2,1)S(1)} %fusion.37), channel_id=1, source_target_pairs={{0,1},{1,0},{2,3},{3,2},{4,5},{5,4},{6,7},{7,6},{8,9},{9,8},{10,11... | collective-permute-start | bytes 49160 | tf_op jit(solution)/shard_map/ppermute | solution.py:8
  34.6 3.1 collective-permute-start.4
  37.5 3.3 copy-start.12
  37.5 3.6 %copy-start.10 = (bf16[1,16,32,256]{3,2,1,0:T(8,128)(2,1)}, bf16[1,16,32,256]{3,2,1,0:T(8,128)(2,1)S(1)}, u32[]{:S(2)}) copy-start(bf16[1,16,32,256]{3,2,1,0:T(8,128)(2,1)S(1)} %get-tuple-element.42) | copy-start | bytes 786436
  37.5 4.6 %copy-start.8 = (bf16[1,16,32,256]{3,2,1,0:T(8,128)(2,1)}, bf16[1,16,32,256]{3,2,1,0:T(8,128)(2,1)S(1)}, u32[]{:S(2)}) copy-start(bf16[1,16,32,256]{3,2,1,0:T(8,128)(2,1)S(1)} %get-tuple-element.41) | copy-start | bytes 786436
  37.5 5.6 %copy-start.6 = (bf16[1,16,32,256]{3,2,1,0:T(8,128)(2,1)}, bf16[1,16,32,256]{3,2,1,0:T(8,128)(2,1)S(1)}, u32[]{:S(2)}) copy-start(bf16[1,16,32,256]{3,2,1,0:T(8,128)(2,1)S(1)} %get-tuple-element.40) | copy-start | bytes 786436
  37.5 6.5 %copy-start.4 = (bf16[1,16,32,256]{3,2,1,0:T(8,128)(2,1)}, bf16[1,16,32,256]{3,2,1,0:T(8,128)(2,1)S(1)}, u32[]{:S(2)}) copy-start(bf16[1,16,32,256]{3,2,1,0:T(8,128)(2,1)S(1)} %get-tuple-element.39) | copy-start | bytes 786436
  37.5 7.5 %copy-start.2 = (bf16[1,16,32,256]{3,2,1,0:T(8,128)(2,1)}, bf16[1,16,32,256]{3,2,1,0:T(8,128)(2,1)S(1)}, u32[]{:S(2)}) copy-start(bf16[1,16,32,256]{3,2,1,0:T(8,128)(2,1)S(1)} %get-tuple-element.38) | copy-start | bytes 786436
  38.8 2.1 copy-start.18
  64.2 67.0 %copy-start = (bf16[256,9,256]{2,0,1:T(8,128)(2,1)}, bf16[256,9,256]{2,0,1:T(8,128)(2,1)S(1)}, u32[]{:S(2)}) copy-start(bf16[256,9,256]{2,0,1:T(8,128)(2,1)S(1)} %reshape.497) | copy-start | bytes 3538948
  64.2 1.7 copy-start.32
  64.4 1.8 copy-start.39
  67.1 1.0 copy-start.11
  67.8 1.0 copy-start.9
  68.1 1.0 copy-start.7
  68.8 1.0 copy-start.5
  69.1 1.0 copy-start.3
  70.5 1.0 copy-start.37
  71.2 1.0 copy-start.36
  72.2 1.0 copy-start.34
  73.2 1.0 copy-start.31
  74.1 1.0 copy-start.29
  74.4 1.1 copy-start.46
  75.1 1.0 copy-start.42
  75.3 4.4 %copy-start.28 = (bf16[1,16,32,256]{3,2,1,0:T(8,128)(2,1)S(1)}, bf16[1,16,32,256]{3,2,1,0:T(8,128)(2,1)}, u32[]{:S(2)}) copy-start(bf16[1,16,32,256]{3,2,1,0:T(8,128)(2,1)} %get-tuple-element.47) | copy-start | bytes 786436
  76.1 3.9 %copy-start.25 = (bf16[1,16,32,256]{3,2,1,0:T(8,128)(2,1)S(1)}, bf16[1,16,32,256]{3,2,1,0:T(8,128)(2,1)}, u32[]{:S(2)}) copy-start(bf16[1,16,32,256]{3,2,1,0:T(8,128)(2,1)} %get-tuple-element.46) | copy-start | bytes 786436
  76.2 15.6 %collective-permute-start.1 = (bf16[2,1,16,32,256]{4,3,2,1,0:T(8,128)(2,1)S(1)}, bf16[2,1,16,32,256]{4,3,2,1,0:T(8,128)(2,1)S(1)}, u32[]{:S(2)}, u32[]{:S(2)}) collective-permute-start(bf16[2,1,16,32,256]{4,3,2,1,0:T(8,128)(2,1)S(1)} %pad_maximum_fusion.1), channel_id=1, source_target_pairs={{0,128},{128,256},{256,384},{1,129},{129,257},{257,385},{2,130},{1... | collective-permute-start | bytes 1572872 | tf_op jit(solution)/shard_map/ppermute | solution.py:14
  80.0 1.0 copy-start.22
  80.7 1.2 copy-start.16
  81.9 9.8 %copy-start.45 = (bf16[2,1,16,32,256]{4,3,2,1,0:T(8,128)(2,1)S(1)}, bf16[2,1,16,32,256]{4,3,2,1,0:T(8,128)(2,1)}, u32[]{:S(2)}) copy-start(bf16[2,1,16,32,256]{4,3,2,1,0:T(8,128)(2,1)} %param.7) | copy-start | bytes 1572868
  82.1 12.0 %copy-start.40 = (bf16[1,1,16,32,256]{4,3,2,0,1:T(8,128)(2,1)S(1)}, bf16[1,1,16,32,256]{4,3,2,0,1:T(8,128)(2,1)}, u32[]{:S(2)}) copy-start(bf16[1,1,16,32,256]{4,3,2,0,1:T(8,128)(2,1)} %get-tuple-element.12) | copy-start | bytes 786436
  82.1 12.0 %copy-start.41 = (bf16[1,1,16,32,256]{4,3,2,0,1:T(8,128)(2,1)S(1)}, bf16[1,1,16,32,256]{4,3,2,0,1:T(8,128)(2,1)}, u32[]{:S(2)}) copy-start(bf16[1,1,16,32,256]{4,3,2,0,1:T(8,128)(2,1)} %get-tuple-element.14) | copy-start | bytes 786436
  91.9 3.9 %collective-permute-start.2 = (bf16[1,32,256]{2,1,0:T(8,128)(2,1)S(1)}, bf16[1,32,256]{2,1,0:T(8,128)(2,1)S(1)}, u32[]{:S(2)}, u32[]{:S(2)}) collective-permute-start(bf16[1,32,256]{2,1,0:T(8,128)(2,1)S(1)} %fusion.38), channel_id=1, source_target_pairs={{0,1},{1,0},{2,3},{3,2},{4,5},{5,4},{6,7},{7,6},{8,9},{9,8},{10,11... | collective-permute-start | bytes 49160 | tf_op jit(solution)/shard_map/ppermute | solution.py:8
  94.3 27.8 %collective-permute-start.5 = (bf16[4,1,16,32,256]{4,3,2,0,1:T(8,128)(2,1)S(1)}, bf16[4,1,16,32,256]{4,3,2,0,1:T(8,128)(2,1)S(1)}, u32[]{:S(2)}, u32[]{:S(2)}) collective-permute-start(bf16[4,1,16,32,256]{4,3,2,0,1:T(8,128)(2,1)S(1)} %pad_maximum_fusion), channel_id=1, source_target_pairs={{128,0},{256,128},{384,256},{129,1},{257,129},{385,257},{130,2},{2... | collective-permute-start | bytes 3145736 | tf_op jit(solution)/shard_map/ppermute | solution.py:14
  98.4 23.7 %copy-start.44 = (bf16[1,1,16,32,256]{4,3,2,0,1:T(8,128)(2,1)S(1)}, bf16[1,1,16,32,256]{4,3,2,0,1:T(8,128)(2,1)}, u32[]{:S(2)}) copy-start(bf16[1,1,16,32,256]{4,3,2,0,1:T(8,128)(2,1)} %get-tuple-element.16) | copy-start | bytes 786436
  98.5 23.7 %copy-start.47 = (bf16[2,1,16,32,256]{4,3,2,1,0:T(8,128)(2,1)S(1)}, bf16[2,1,16,32,256]{4,3,2,1,0:T(8,128)(2,1)}, u32[]{:S(2)}) copy-start(bf16[2,1,16,32,256]{4,3,2,1,0:T(8,128)(2,1)} %param.8) | copy-start | bytes 1572868
  123.1 4.3 %collective-permute-start.7 = (bf16[1,32,256]{2,1,0:T(8,128)(2,1)S(1)}, bf16[1,32,256]{2,1,0:T(8,128)(2,1)S(1)}, u32[]{:S(2)}, u32[]{:S(2)}) collective-permute-start(bf16[1,32,256]{2,1,0:T(8,128)(2,1)S(1)} %fusion.34), channel_id=1, source_target_pairs={{0,1},{1,0},{2,3},{3,2},{4,5},{5,4},{6,7},{7,6},{8,9},{9,8},{10,11... | collective-permute-start | bytes 49160 | tf_op jit(solution)/shard_map/ppermute | solution.py:8
  125.0 5.1 %collective-permute-start.6 = (bf16[1,32,256]{2,1,0:T(8,128)(2,1)S(1)}, bf16[1,32,256]{2,1,0:T(8,128)(2,1)S(1)}, u32[]{:S(2)}, u32[]{:S(2)}) collective-permute-start(bf16[1,32,256]{2,1,0:T(8,128)(2,1)S(1)} %fusion.35), channel_id=1, source_target_pairs={{0,1},{1,0},{2,3},{3,2},{4,5},{5,4},{6,7},{7,6},{8,9},{9,8},{10,11... | collective-permute-start | bytes 49160 | tf_op jit(solution)/shard_map/ppermute | solution.py:8
  145.8 1.3 copy-start.1
  145.8 2.5 copy-start.27
  147.1 1.5 copy-start.24
  149.2 1.0 copy-start.26
  149.9 1.0 copy-start.21
  150.2 1.1 copy-start.14
  (10 other events, 9.3 us)
Sparse Core Ops, SparseCore 0:
  146.0 197.2 all-reduce.7
